TPU v7x, 32 devices: a whole 2x2x4 slice. The times are simulated.
32 devices in a mesh: station: 8 (over y, x, core), tm: 4 (over z).
Axes of the slice: x: 2, y: 2, z: 4, core: 2. Of those that a mesh axis runs over, the one named last changes fastest.
Arguments:
- samples: bfloat16 [64, 256, 2048], P('tm', 'station'), may hold values from -6 to 6
- history: bfloat16 [15, 256, 2048], P(None, 'station'), may hold values from -6 to 6
- taps: float32 [16, 2048], replicated, may hold values from -0.03125 to 0.03125
Outputs:
- visibility: float32 [1024, 2, 256, 256], P(('station', 'tm'))
- beam_power: float32 [64, 1024], P('tm', 'station')
All inputs are finite; a program needn't handle non-finite values.
Results may differ from a plain program's by a relative error of at most 0.0095.
Values may be sent and summed in bfloat16 or wider, within the bound.
A program may use at most 128 MiB of HBM per device.

v0:
```python
import math
import jax
import jax.numpy as jnp
from jax import lax
from jax.sharding import PartitionSpec as P


def passed_along(block, axis, distance):
    devices = range(lax.axis_size(axis))
    route = [(i - distance, i) for i in devices if i - distance in devices]
    return lax.ppermute(block, axis, route)


def dft_parts(frame_len, channels):
    sample_index = jnp.arange(frame_len, dtype=jnp.int32)
    channel_index = jnp.arange(channels, dtype=jnp.int32)
    phases = sample_index[:, None] * channel_index[None, :] % frame_len
    angles = phases.astype(jnp.float32) * (2.0 * math.pi / frame_len)
    return (jnp.cos(angles).astype(jnp.bfloat16), (-jnp.sin(angles)).astype(jnp.bfloat16))


def filter_frames(extended, taps, frames_out):
    span_taps = taps.shape[0]
    running = jnp.zeros((frames_out,) + extended.shape[1:], jnp.float32)
    for tap_index in range(span_taps):
        offset = span_taps - 1 - tap_index
        running = running + taps[tap_index][None, None, :] * extended[
            offset : offset + frames_out
        ].astype(jnp.float32)
    return jnp.swapaxes(running, 0, 1).astype(jnp.bfloat16)


def power_of(grouped):
    values = grouped.astype(jnp.float32)
    return jnp.sum(values * values, axis=(-3, -2)) * (1.0 / grouped.shape[-3])


def flat_pair(piece):
    chan_count, input_count, pair_count, frame_count = piece.shape
    flat = piece.reshape(chan_count, input_count, pair_count * frame_count)
    rotated = jnp.concatenate([-piece[:, :, 1:2], piece[:, :, 0:1]], axis=2)
    return (flat, rotated.reshape(chan_count, input_count, pair_count * frame_count))


def correlate(piece, norm_scale):
    flat, rotated = flat_pair(piece)
    real_part = (
        jnp.einsum("cak,cbk->cab", flat, flat, preferred_element_type=jnp.float32) * norm_scale
    )
    imag_part = (
        jnp.einsum("cak,cbk->cab", rotated, flat, preferred_element_type=jnp.float32) * norm_scale
    )
    return (real_part, imag_part)


def body(samples, history, taps):
    frames_dev = samples.shape[0]
    frame_len = samples.shape[2]
    span_taps = taps.shape[0]
    cos_part, sin_part = dft_parts(frame_len, frame_len // 2)
    tail_block = samples[frames_dev - (span_taps - 1) :]
    prior_frames = passed_along(tail_block, "tm", 1)
    prior_frames = jnp.where(lax.axis_index("tm") == 0, history, prior_frames)
    extended = jnp.concatenate([prior_frames, samples], axis=0)
    weighted = filter_frames(extended, taps, frames_dev)
    real_spec = jnp.einsum("nc,atn->cat", cos_part, weighted, preferred_element_type=jnp.float32)
    imag_spec = jnp.einsum("nc,atn->cat", sin_part, weighted, preferred_element_type=jnp.float32)
    spectra = jnp.stack([real_spec, imag_spec], axis=2).astype(jnp.bfloat16)
    time_groups = lax.axis_size("tm")
    norm_scale = 1.0 / (frames_dev * time_groups)
    gathered = lax.all_to_all(
        lax.all_to_all(spectra[None], "station", split_axis=1, concat_axis=2, tiled=True),
        "tm",
        split_axis=1,
        concat_axis=0,
        tiled=True,
    )
    own_channels = gathered.shape[1]
    inputs = gathered.shape[2]
    power_own = power_of(gathered)
    power_back = lax.all_to_all(power_own, "tm", split_axis=0, concat_axis=1, tiled=True)
    power_rows = jnp.transpose(power_back[0])

    def accumulate(block_index, running):
        time_piece = lax.dynamic_index_in_dim(gathered, block_index, 0, keepdims=False)
        real_part, imag_part = correlate(time_piece, norm_scale)
        partial_value = jnp.stack([real_part, imag_part], axis=1).astype(jnp.bfloat16)
        partial_value = lax.optimization_barrier(partial_value)
        return running + partial_value.astype(jnp.float32)

    initial_sum = jnp.zeros((own_channels, 2, inputs, inputs), jnp.float32)
    visibility = lax.fori_loop(0, time_groups, accumulate, initial_sum)
    return (visibility, power_rows)


def solution(mesh):
    return jax.shard_map(
        body,
        mesh=mesh,
        in_specs=(P("tm", "station", None), P(None, "station", None), P()),
        out_specs=(P(("station", "tm"), None, None, None), P("tm", "station")),
        check_vma=False,
    )
```

profile of v0, /device:TPU:0, one launch (start us, length us, event | category | flops | bytes accessed | tf_op | source)
XLA Modules:
  0.0 371.6 jit_solution(146463902237839219)
XLA Ops:
  3.8 6.2 %collective-permute-start = (bf16[15,32,2048]{2,1,0:T(8,128)(2,1)}, bf16[15,32,2048]{2,1,0:T(8,128)(2,1)}, u32[]{:S(2)}, u32[]{:S(2)}) collective-permute-start(bf16[15,32,2048]{2,1,0:T(8,128)(2,1)} %slice.112), channel_id=1, source_target_pairs={{0,1},{1,2},{2,3},{4,5},{5,6},{6,7},{8,9},{9,10},{10,11},{12,13},{... | collective-permute-start | bytes 5898248 | tf_op jit(solution)/shard_map/ppermute | solution.py:11
  11.7 39.5 %collective-permute-done = bf16[15,32,2048]{2,1,0:T(8,128)(2,1)} collective-permute-done((bf16[15,32,2048]{2,1,0:T(8,128)(2,1)}, bf16[15,32,2048]{2,1,0:T(8,128)(2,1)}, u32[]{:S(2)}, u32[]{:S(2)}) %collective-permute-start) | collective-permute-done | bytes 1966112 | tf_op jit(solution)/shard_map/ppermute | solution.py:11
  52.9 9.5 %add_convert_fusion = bf16[16,32,2048]{2,1,0:T(8,128)(2,1)S(1)} fusion(bf16[16,32,2048]{2,1,0:T(8,128)(2,1)S(1)} %copy-done, bf16[15,32,2048]{2,1,0:T(8,128)(2,1)S(1)} %broadcast_select_fusion, f32[2048]{0:T(1024)S(1)} %bitcast.116, f32[2048]{0:T(1024)S(1)} %bitcast.117, f32[2048]{0:T(1024)S(1)} %bitcast.103, f32[2048]{0:T(1024)S(1)} %bitcast.104, ...), kind=kLoop, calls=%fused_computation.53 | loop fusion | flops 66060288 | bytes 6291456 | tf_op jit(solution)/shard_map/convert_element_type | solution.py:30
  62.4 31.8 %fusion.42 = bf16[1,1024,32,1,16]{1,2,4,3,0:T(8,128)(2,1)S(1)} fusion(bf16[16,32,2048]{2,1,0:T(8,128)(2,1)S(1)} %add_convert_fusion), kind=kOutput, calls=%fused_computation.75 | convolution fusion | flops 2179465216 | bytes 3145728 | tf_op jit(solution)/shard_map/nc,atn->cat/dot_general | solution.py:66
  94.2 32.5 %fusion.47 = bf16[1,1024,32,1,16]{1,2,4,3,0:T(8,128)(2,1)S(1)} fusion(bf16[16,32,2048]{2,1,0:T(8,128)(2,1)S(1)} %add_convert_fusion), kind=kOutput, calls=%fused_computation.76 | convolution fusion | flops 2181562368 | bytes 3145728 | tf_op jit(solution)/shard_map/nc,atn->cat/dot_general | solution.py:67
  126.8 12.1 %copy.33 = bf16[1,1024,32,2,16]{2,4,3,0,1:T(8,128)(2,1)} copy(bf16[1,1024,32,2,16]{1,2,4,3,0:T(8,128)(2,1)S(1)} %pad_maximum_fusion.3) | data formatting | bytes 4194304 | tf_op jit(solution)/shard_map/stack | solution.py:68
  138.9 10.1 %reshape.82 = bf16[8,2,65536]{2,1,0:T(2,128)(2,1)S(1)} reshape(bf16[1024,1,2,16,32]{4,3,2,1,0:T(8,128)(2,1)} %bitcast.96) | data formatting | bytes 4194304
  149.1 30.2 %all_to_all.39 = bf16[8,2,65536]{2,1,0:T(2,128)(2,1)} all-to-all(bf16[8,2,65536]{2,1,0:T(2,128)(2,1)S(1)} %reshape.82), channel_id=1, replica_groups=mesh['station'=8,'tm'=4] {'station'}, dimensions={0} | all-to-all | bytes 4194304 | tf_op jit(solution)/shard_map/all_to_all | solution.py:72
  179.3 8.6 %reshape.83 = bf16[1024,1,2,16,32]{4,3,2,1,0:T(8,128)(2,1)} reshape(bf16[8,2,65536]{2,1,0:T(2,128)(2,1)} %all_to_all.39) | data formatting | bytes 4194304
  187.9 9.3 %copy.42 = bf16[1,8,128,32,2,16]{2,1,5,4,3,0:T(8,128)(2,1)S(1)} copy(bf16[1,8,128,32,2,16]{3,5,4,2,1,0:T(8,128)(2,1)} %bitcast.97) | data formatting | bytes 4194304 | tf_op jit(solution)/shard_map/all_to_all | solution.py:72
  198.9 4.9 %copy.36 = bf16[1,128,256,2,16]{2,4,3,0,1:T(8,128)(2,1)} copy(bf16[1,128,256,2,16]{1,4,3,2,0:T(8,128)(2,1)} %bitcast.99) | data formatting | bytes 4194304 | tf_op jit(solution)/shard_map/all_to_all | solution.py:72
  203.8 5.8 %all-to-all-start.1 = ((bf16[1,128,256,2,16]{2,4,3,0,1:T(8,128)(2,1)}), bf16[1,128,256,2,16]{2,4,3,0,1:T(8,128)(2,1)S(1)}, u32[]{:S(2)}, u32[]{:S(2)}) async-start(bf16[1,128,256,2,16]{2,4,3,0,1:T(8,128)(2,1)} %copy.36), calls=%async_computation.1 | async-start | bytes 4194304 | tf_op jit(solution)/shard_map/all_to_all | solution.py:71
  209.6 47.5 %all-to-all-done.1 = bf16[1,128,256,2,16]{2,4,3,0,1:T(8,128)(2,1)S(1)} async-done(((bf16[1,128,256,2,16]{2,4,3,0,1:T(8,128)(2,1)}), bf16[1,128,256,2,16]{2,4,3,0,1:T(8,128)(2,1)S(1)}, u32[]{:S(2)}, u32[]{:S(2)}) %all-to-all-start.1) | async-done | bytes 2097184 | tf_op jit(solution)/shard_map/all_to_all | solution.py:71
  258.4 3.2 all-to-all-start.2
  261.7 96.2 %while.14 = (s32[]{:T(128)}, f32[32,2,256,256]{3,2,0,1:T(8,128)}, bf16[4,32,256,2,16]{2,4,3,1,0:T(8,128)(2,1)S(1)}, s32[]{:T(128)}, s32[]{:T(128)}) while((s32[]{:T(128)}, f32[32,2,256,256]{3,2,0,1:T(8,128)}, bf16[4,32,256,2,16]{2,4,3,1,0:T(8,128)(2,1)S(1)}, s32[]{:T(128)}, s32[]{:T(128)}) %tuple.65), condition=%wide.region_1.2_spmd.clone, body=%wide.region_0.1_spmd.clone.sunk | while | flops 293994496 | bytes 72876112 | solution.py:92
  266.4 6.3 %pad_maximum_fusion.7 = bf16[32,2,256,256]{3,2,0,1:T(8,128)(2,1)} fusion(bf16[32,1,256,256]{3,2,0,1:T(8,128)(2,1)S(1)} %fusion.78, bf16[32,1,256,256]{3,2,0,1:T(8,128)(2,1)} %fusion.79), kind=kLoop, calls=%fused_computation.1.clone.1 | loop fusion | flops 4194304 | bytes 16777216 | tf_op jit(solution)/shard_map/while/body/eval_jaxpr/stack | solution.py:87
  272.8 9.9 %select_add_fusion.2 = f32[32,2,256,256]{3,2,0,1:T(8,128)} fusion(f32[32,2,256,256]{3,2,0,1:T(8,128)} %get-tuple-element.149, bf16[32,2,256,256]{3,2,0,1:T(8,128)(2,1)} %pad_maximum_fusion.7, pred[]{:T(512)S(6)} %compare.4), kind=kLoop, calls=%fused_computation.clone.1 | loop fusion | flops 12582912 | bytes 41943040 | tf_op jit(solution)/shard_map/while/body/eval_jaxpr/add | solution.py:89
  287.5 6.3 %pad_maximum_fusion.7 = bf16[32,2,256,256]{3,2,0,1:T(8,128)(2,1)} fusion(bf16[32,1,256,256]{3,2,0,1:T(8,128)(2,1)S(1)} %fusion.78, bf16[32,1,256,256]{3,2,0,1:T(8,128)(2,1)} %fusion.79), kind=kLoop, calls=%fused_computation.1.clone.1 | loop fusion | flops 4194304 | bytes 16777216 | tf_op jit(solution)/shard_map/while/body/eval_jaxpr/stack | solution.py:87
  293.8 14.0 %select_add_fusion.2 = f32[32,2,256,256]{3,2,0,1:T(8,128)} fusion(f32[32,2,256,256]{3,2,0,1:T(8,128)} %get-tuple-element.149, bf16[32,2,256,256]{3,2,0,1:T(8,128)(2,1)} %pad_maximum_fusion.7, pred[]{:T(512)S(6)} %compare.4), kind=kLoop, calls=%fused_computation.clone.1 | loop fusion | flops 12582912 | bytes 41943040 | tf_op jit(solution)/shard_map/while/body/eval_jaxpr/add | solution.py:89
  312.5 6.3 %pad_maximum_fusion.7 = bf16[32,2,256,256]{3,2,0,1:T(8,128)(2,1)} fusion(bf16[32,1,256,256]{3,2,0,1:T(8,128)(2,1)S(1)} %fusion.78, bf16[32,1,256,256]{3,2,0,1:T(8,128)(2,1)} %fusion.79), kind=kLoop, calls=%fused_computation.1.clone.1 | loop fusion | flops 4194304 | bytes 16777216 | tf_op jit(solution)/shard_map/while/body/eval_jaxpr/stack | solution.py:87
  318.9 14.0 %select_add_fusion.2 = f32[32,2,256,256]{3,2,0,1:T(8,128)} fusion(f32[32,2,256,256]{3,2,0,1:T(8,128)} %get-tuple-element.149, bf16[32,2,256,256]{3,2,0,1:T(8,128)(2,1)} %pad_maximum_fusion.7, pred[]{:T(512)S(6)} %compare.4), kind=kLoop, calls=%fused_computation.clone.1 | loop fusion | flops 12582912 | bytes 41943040 | tf_op jit(solution)/shard_map/while/body/eval_jaxpr/add | solution.py:89
  337.6 6.3 %pad_maximum_fusion.7 = bf16[32,2,256,256]{3,2,0,1:T(8,128)(2,1)} fusion(bf16[32,1,256,256]{3,2,0,1:T(8,128)(2,1)S(1)} %fusion.78, bf16[32,1,256,256]{3,2,0,1:T(8,128)(2,1)} %fusion.79), kind=kLoop, calls=%fused_computation.1.clone.1 | loop fusion | flops 4194304 | bytes 16777216 | tf_op jit(solution)/shard_map/while/body/eval_jaxpr/stack | solution.py:87
  343.9 14.0 %select_add_fusion.2 = f32[32,2,256,256]{3,2,0,1:T(8,128)} fusion(f32[32,2,256,256]{3,2,0,1:T(8,128)} %get-tuple-element.149, bf16[32,2,256,256]{3,2,0,1:T(8,128)(2,1)} %pad_maximum_fusion.7, pred[]{:T(512)S(6)} %compare.4), kind=kLoop, calls=%fused_computation.clone.1 | loop fusion | flops 12582912 | bytes 41943040 | tf_op jit(solution)/shard_map/while/body/eval_jaxpr/add | solution.py:89
  357.9 11.7 %copy.41 = f32[32,2,256,256]{3,2,1,0:T(8,128)} copy(f32[32,2,256,256]{3,2,0,1:T(8,128)} %get-tuple-element.94) | data formatting | bytes 33554432
  (44 shorter events, 30.5 us)
Async XLA Ops:
  0.6 52.3 %copy-start = (bf16[16,32,2048]{2,1,0:T(8,128)(2,1)S(1)}, bf16[16,32,2048]{2,1,0:T(8,128)(2,1)}, u32[]{:S(2)}) copy-start(bf16[16,32,2048]{2,1,0:T(8,128)(2,1)} %param.5) | copy-start | bytes 6291460
  3.8 47.3 %collective-permute-start = (bf16[15,32,2048]{2,1,0:T(8,128)(2,1)}, bf16[15,32,2048]{2,1,0:T(8,128)(2,1)}, u32[]{:S(2)}, u32[]{:S(2)}) collective-permute-start(bf16[15,32,2048]{2,1,0:T(8,128)(2,1)} %slice.112), channel_id=1, source_target_pairs={{0,1},{1,2},{2,3},{4,5},{5,6},{6,7},{8,9},{9,10},{10,11},{12,13},{... | collective-permute-start | bytes 5898248 | tf_op jit(solution)/shard_map/ppermute | solution.py:11
  203.8 53.3 %all-to-all-start.1 = ((bf16[1,128,256,2,16]{2,4,3,0,1:T(8,128)(2,1)}), bf16[1,128,256,2,16]{2,4,3,0,1:T(8,128)(2,1)S(1)}, u32[]{:S(2)}, u32[]{:S(2)}) async-start(bf16[1,128,256,2,16]{2,4,3,0,1:T(8,128)(2,1)} %copy.36), calls=%async_computation.1 | async-start | bytes 4194304 | tf_op jit(solution)/shard_map/all_to_all | solution.py:71
  258.4 111.2 %all-to-all-start.2 = ((f32[4,1,512]{2,1,0:T(1,128)}), f32[4,1,512]{2,1,0:T(1,128)S(1)}, u32[]{:S(2)}, u32[]{:S(2)}) async-start(f32[4,1,512]{2,1,0:T(1,128)} %reshape.84), calls=%async_computation.2 | async-start | bytes 16384 | tf_op jit(solution)/shard_map/all_to_all | solution.py:81
where the time goes:
time: 373 us; the launch traced here: 372 us
  other arithmetic  90.2 us (24%)
  waiting for transfers between devices  87 us (23%)
  matrix products  82.4 us (22%)
  local copies, waits for them, and re-layouts  65.6 us (18%)
  blocking collectives  30.2 us (8%)
  starting transfers between devices  15.2 us (4%)
    add x4, other arithmetic, accumulate(): return running + partial_value.astype(jnp.float32)  51.9 us
    all_to_all x1, waiting for transfers between devices, body(): lax.all_to_all(lax.all_to_all(spectra[None], 'station', split_axis=1, con...  47.5 us
    ppermute x1, waiting for transfers between devices, passed_along(): return lax.ppermute(block, axis, route)  39.5 us
    dot_general x1, matrix products, body(): jnp.einsum('nc,atn->cat', sin_part, weighted, preferred_element_type=jnp....  32.5 us
    dot_general x1, matrix products, body(): jnp.einsum('nc,atn->cat', cos_part, weighted, preferred_element_type=jnp....  31.8 us
    unnamed x7, local copies, waits for them, and re-layouts  31.2 us
    all_to_all x1, blocking collectives, body(): lax.all_to_all(spectra[None], 'station', split_axis=1, concat_axis=2, til...  30.2 us
    another operation x4, other arithmetic, accumulate(): jnp.stack([real_part, imag_part], axis=1).astype(jnp.bfloat16)  25.4 us
  transfers between devices with their start and end apart: 3, of which 2 were waited for; matrix products, arithmetic and copies ran while one was open for 29% of the time, Pallas kernels for 0%

commit v1 on v0

--- a/solution.py
+++ b/solution.py
@@ -68,12 +68,17 @@
     spectra = jnp.stack([real_spec, imag_spec], axis=2).astype(jnp.bfloat16)
     time_groups = lax.axis_size("tm")
     norm_scale = 1.0 / (frames_dev * time_groups)
+
+    def _connect_keys(buf, comm_axis):
+        extra = lax.axis_size(comm_axis)
+        item_now = jnp.split(buf, extra, 1)
+        latest = jnp.stack(item_now)
+        last = lax.all_to_all(latest, axis_name=comm_axis, concat_axis=0, split_axis=0)
+        placed = jnp.concatenate(last, axis=2)
+        return placed
+
     gathered = lax.all_to_all(
-        lax.all_to_all(spectra[None], "station", split_axis=1, concat_axis=2, tiled=True),
-        "tm",
-        split_axis=1,
-        concat_axis=0,
-        tiled=True,
+        _connect_keys(spectra[None], "station"), "tm", split_axis=1, concat_axis=0, tiled=True
     )
     own_channels = gathered.shape[1]
     inputs = gathered.shape[2]

time: 373 us -> 333 us (0.89)
  local copies, waits for them, and re-layouts: 65.6 us -> 26 us
    unnamed x7 -> x5, local copies, waits for them, and re-layouts: 31.2 us -> 12.4 us
    all_to_all x3 -> x0, local copies, waits for them, and re-layouts: 15.9 us -> none  [body(): lax.all_to_all(spectra[None], 'station', split_axis=1, concat_axis=2, til...]
    another operation x1 -> x0, local copies, waits for them, and re-layouts: 12.1 us -> none  [body(): spectra = jnp.stack([real_spec, imag_spec], axis=2).astype(jnp.bfloat16)]
    reshape x0 -> x2, local copies, waits for them, and re-layouts: none -> 7.05 us  [_connect_keys(): placed = jnp.concatenate(last, axis=2)]
  transfers between devices with their start and end apart: 3 -> 3, of which waited for: 2 -> 2; matrix products, arithmetic and copies ran while one was open for 29% -> 33% of each run, Pallas kernels for 0% -> 0%
where the time goes in v1:
time: 333 us
  other arithmetic  90.6 us (27%)
  waiting for transfers between devices  87 us (26%)
  matrix products  82.4 us (25%)
  blocking collectives  30.1 us (9%)
  local copies, waits for them, and re-layouts  26 us (8%)
  starting transfers between devices  15.5 us (5%)
    add x4, other arithmetic, accumulate(): return running + partial_value.astype(jnp.float32)  51.9 us
    all_to_all x1, waiting for transfers between devices, body(): lax.all_to_all(_connect_keys(spectra[None], 'station'), 'tm', split_axis=...  47.5 us
    ppermute x1, waiting for transfers between devices, passed_along(): return lax.ppermute(block, axis, route)  39.5 us
    dot_general x1, matrix products, body(): jnp.einsum('nc,atn->cat', sin_part, weighted, preferred_element_type=jnp....  32.5 us
    dot_general x1, matrix products, body(): jnp.einsum('nc,atn->cat', cos_part, weighted, preferred_element_type=jnp....  31.8 us
    all_to_all x1, blocking collectives, _connect_keys(): lax.all_to_all(latest, axis_name=comm_axis, concat_axis=0, split_axis=0)  30.1 us
    another operation x4, other arithmetic, accumulate(): jnp.stack([real_part, imag_part], axis=1).astype(jnp.bfloat16)  25.4 us
    dot_general x4, matrix products, correlate(): jnp.einsum('cak,cbk->cab', flat, flat, preferred_element_type=jnp.float32)  13 us
  transfers between devices with their start and end apart: 3, of which 2 were waited for; matrix products, arithmetic and copies ran while one was open for 33% of the time, Pallas kernels for 0%

profile of v1, /device:TPU:0, one launch (start us, length us, event | category | flops | bytes accessed | tf_op | source)
XLA Modules:
  0.0 332.5 jit_solution(14042927272661791361)
XLA Ops:
  3.8 6.2 %collective-permute-start = (bf16[15,32,2048]{2,1,0:T(8,128)(2,1)}, bf16[15,32,2048]{2,1,0:T(8,128)(2,1)}, u32[]{:S(2)}, u32[]{:S(2)}) collective-permute-start(bf16[15,32,2048]{2,1,0:T(8,128)(2,1)} %slice.112), channel_id=1, source_target_pairs={{0,1},{1,2},{2,3},{4,5},{5,6},{6,7},{8,9},{9,10},{10,11},{12,13},{... | collective-permute-start | bytes 5898248 | tf_op jit(solution)/shard_map/ppermute | solution.py:11
  11.7 39.5 %collective-permute-done = bf16[15,32,2048]{2,1,0:T(8,128)(2,1)} collective-permute-done((bf16[15,32,2048]{2,1,0:T(8,128)(2,1)}, bf16[15,32,2048]{2,1,0:T(8,128)(2,1)}, u32[]{:S(2)}, u32[]{:S(2)}) %collective-permute-start) | collective-permute-done | bytes 1966112 | tf_op jit(solution)/shard_map/ppermute | solution.py:11
  52.9 9.5 %add_convert_fusion = bf16[16,32,2048]{2,1,0:T(8,128)(2,1)S(1)} fusion(bf16[16,32,2048]{2,1,0:T(8,128)(2,1)S(1)} %copy-done, bf16[15,32,2048]{2,1,0:T(8,128)(2,1)S(1)} %broadcast_select_fusion, f32[2048]{0:T(1024)S(1)} %bitcast.129, f32[2048]{0:T(1024)S(1)} %bitcast.130, f32[2048]{0:T(1024)S(1)} %bitcast.116, f32[2048]{0:T(1024)S(1)} %bitcast.117, ...), kind=kLoop, calls=%fused_computation.53 | loop fusion | flops 66060288 | bytes 6291456 | tf_op jit(solution)/shard_map/convert_element_type | solution.py:30
  62.4 31.8 %fusion.42 = bf16[1,1024,32,1,16]{1,2,4,3,0:T(8,128)(2,1)S(1)} fusion(bf16[16,32,2048]{2,1,0:T(8,128)(2,1)S(1)} %add_convert_fusion), kind=kOutput, calls=%fused_computation.88 | convolution fusion | flops 2179465216 | bytes 3145728 | tf_op jit(solution)/shard_map/nc,atn->cat/dot_general | solution.py:66
  94.2 32.5 %fusion.47 = bf16[1,1024,32,1,16]{1,2,4,3,0:T(8,128)(2,1)S(1)} fusion(bf16[16,32,2048]{2,1,0:T(8,128)(2,1)S(1)} %add_convert_fusion), kind=kOutput, calls=%fused_computation.89 | convolution fusion | flops 2181562368 | bytes 3145728 | tf_op jit(solution)/shard_map/nc,atn->cat/dot_general | solution.py:67
  127.4 30.1 %all_to_all.26 = bf16[8,1,128,32,2,16]{2,3,5,4,1,0:T(8,128)(2,1)S(1)} all-to-all(bf16[8,1,128,32,2,16]{2,3,5,4,1,0:T(8,128)(2,1)S(1)} %fusion.60), channel_id=1, replica_groups=mesh['station'=8,'tm'=4] {'station'}, dimensions={0} | all-to-all | bytes 4194304 | tf_op jit(solution)/shard_map/all_to_all | solution.py:76
  159.6 4.9 %copy.30 = bf16[1,128,256,2,16]{2,4,3,0,1:T(8,128)(2,1)} copy(bf16[1,128,256,2,16]{1,4,3,2,0:T(8,128)(2,1)} %bitcast.112) | data formatting | bytes 4194304 | tf_op jit(solution)/shard_map/reshape | solution.py:77
  164.5 5.8 %all-to-all-start.1 = ((bf16[1,128,256,2,16]{2,4,3,0,1:T(8,128)(2,1)}), bf16[1,128,256,2,16]{2,4,3,0,1:T(8,128)(2,1)S(1)}, u32[]{:S(2)}, u32[]{:S(2)}) async-start(bf16[1,128,256,2,16]{2,4,3,0,1:T(8,128)(2,1)} %copy.30), calls=%async_computation.1 | async-start | bytes 4194304 | tf_op jit(solution)/shard_map/all_to_all | solution.py:80
  170.3 47.5 %all-to-all-done.1 = bf16[1,128,256,2,16]{2,4,3,0,1:T(8,128)(2,1)S(1)} async-done(((bf16[1,128,256,2,16]{2,4,3,0,1:T(8,128)(2,1)}), bf16[1,128,256,2,16]{2,4,3,0,1:T(8,128)(2,1)S(1)}, u32[]{:S(2)}, u32[]{:S(2)}) %all-to-all-start.1) | async-done | bytes 2097184 | tf_op jit(solution)/shard_map/all_to_all | solution.py:80
  219.2 3.5 %all-to-all-start.2 = ((f32[4,1,512]{2,1,0:T(1,128)}), f32[4,1,512]{2,1,0:T(1,128)S(1)}, u32[]{:S(2)}, u32[]{:S(2)}) async-start(f32[4,1,512]{2,1,0:T(1,128)} %reshape.90), calls=%async_computation.2 | async-start | bytes 16384 | tf_op jit(solution)/shard_map/all_to_all | solution.py:86
  222.6 96.2 %while.14 = (s32[]{:T(128)}, f32[32,2,256,256]{3,2,0,1:T(8,128)}, bf16[4,32,256,2,16]{2,4,3,1,0:T(8,128)(2,1)S(1)}, s32[]{:T(128)}, s32[]{:T(128)}) while((s32[]{:T(128)}, f32[32,2,256,256]{3,2,0,1:T(8,128)}, bf16[4,32,256,2,16]{2,4,3,1,0:T(8,128)(2,1)S(1)}, s32[]{:T(128)}, s32[]{:T(128)}) %tuple.65), condition=%wide.region_1.2_spmd.clone, body=%wide.region_0.1_spmd.clone.sunk | while | flops 293994496 | bytes 72876112 | solution.py:97
  224.2 3.2 fusion.88
  227.4 6.3 %pad_maximum_fusion.7 = bf16[32,2,256,256]{3,2,0,1:T(8,128)(2,1)} fusion(bf16[32,1,256,256]{3,2,0,1:T(8,128)(2,1)S(1)} %fusion.87, bf16[32,1,256,256]{3,2,0,1:T(8,128)(2,1)} %fusion.88), kind=kLoop, calls=%fused_computation.1.clone.1 | loop fusion | flops 4194304 | bytes 16777216 | tf_op jit(solution)/shard_map/while/body/eval_jaxpr/stack | solution.py:92
  233.8 9.9 %select_add_fusion.2 = f32[32,2,256,256]{3,2,0,1:T(8,128)} fusion(f32[32,2,256,256]{3,2,0,1:T(8,128)} %get-tuple-element.149, bf16[32,2,256,256]{3,2,0,1:T(8,128)(2,1)} %pad_maximum_fusion.7, pred[]{:T(512)S(6)} %compare.4), kind=kLoop, calls=%fused_computation.clone.1 | loop fusion | flops 12582912 | bytes 41943040 | tf_op jit(solution)/shard_map/while/body/eval_jaxpr/add | solution.py:94
  245.2 3.2 fusion.88
  248.4 6.3 %pad_maximum_fusion.7 = bf16[32,2,256,256]{3,2,0,1:T(8,128)(2,1)} fusion(bf16[32,1,256,256]{3,2,0,1:T(8,128)(2,1)S(1)} %fusion.87, bf16[32,1,256,256]{3,2,0,1:T(8,128)(2,1)} %fusion.88), kind=kLoop, calls=%fused_computation.1.clone.1 | loop fusion | flops 4194304 | bytes 16777216 | tf_op jit(solution)/shard_map/while/body/eval_jaxpr/stack | solution.py:92
  254.8 14.0 %select_add_fusion.2 = f32[32,2,256,256]{3,2,0,1:T(8,128)} fusion(f32[32,2,256,256]{3,2,0,1:T(8,128)} %get-tuple-element.149, bf16[32,2,256,256]{3,2,0,1:T(8,128)(2,1)} %pad_maximum_fusion.7, pred[]{:T(512)S(6)} %compare.4), kind=kLoop, calls=%fused_computation.clone.1 | loop fusion | flops 12582912 | bytes 41943040 | tf_op jit(solution)/shard_map/while/body/eval_jaxpr/add | solution.py:94
  270.2 3.2 fusion.88
  273.5 6.3 %pad_maximum_fusion.7 = bf16[32,2,256,256]{3,2,0,1:T(8,128)(2,1)} fusion(bf16[32,1,256,256]{3,2,0,1:T(8,128)(2,1)S(1)} %fusion.87, bf16[32,1,256,256]{3,2,0,1:T(8,128)(2,1)} %fusion.88), kind=kLoop, calls=%fused_computation.1.clone.1 | loop fusion | flops 4194304 | bytes 16777216 | tf_op jit(solution)/shard_map/while/body/eval_jaxpr/stack | solution.py:92
  279.8 14.0 %select_add_fusion.2 = f32[32,2,256,256]{3,2,0,1:T(8,128)} fusion(f32[32,2,256,256]{3,2,0,1:T(8,128)} %get-tuple-element.149, bf16[32,2,256,256]{3,2,0,1:T(8,128)(2,1)} %pad_maximum_fusion.7, pred[]{:T(512)S(6)} %compare.4), kind=kLoop, calls=%fused_computation.clone.1 | loop fusion | flops 12582912 | bytes 41943040 | tf_op jit(solution)/shard_map/while/body/eval_jaxpr/add | solution.py:94
  295.3 3.2 fusion.88
  298.6 6.3 %pad_maximum_fusion.7 = bf16[32,2,256,256]{3,2,0,1:T(8,128)(2,1)} fusion(bf16[32,1,256,256]{3,2,0,1:T(8,128)(2,1)S(1)} %fusion.87, bf16[32,1,256,256]{3,2,0,1:T(8,128)(2,1)} %fusion.88), kind=kLoop, calls=%fused_computation.1.clone.1 | loop fusion | flops 4194304 | bytes 16777216 | tf_op jit(solution)/shard_map/while/body/eval_jaxpr/stack | solution.py:92
  304.9 14.0 %select_add_fusion.2 = f32[32,2,256,256]{3,2,0,1:T(8,128)} fusion(f32[32,2,256,256]{3,2,0,1:T(8,128)} %get-tuple-element.149, bf16[32,2,256,256]{3,2,0,1:T(8,128)(2,1)} %pad_maximum_fusion.7, pred[]{:T(512)S(6)} %compare.4), kind=kLoop, calls=%fused_computation.clone.1 | loop fusion | flops 12582912 | bytes 41943040 | tf_op jit(solution)/shard_map/while/body/eval_jaxpr/add | solution.py:94
  318.9 11.7 %copy.35 = f32[32,2,256,256]{3,2,1,0:T(8,128)} copy(f32[32,2,256,256]{3,2,0,1:T(8,128)} %get-tuple-element.94) | data formatting | bytes 33554432
  (47 shorter events, 18.5 us)
Async XLA Ops:
  0.6 52.3 %copy-start = (bf16[16,32,2048]{2,1,0:T(8,128)(2,1)S(1)}, bf16[16,32,2048]{2,1,0:T(8,128)(2,1)}, u32[]{:S(2)}) copy-start(bf16[16,32,2048]{2,1,0:T(8,128)(2,1)} %param.5) | copy-start | bytes 6291460
  3.8 47.3 %collective-permute-start = (bf16[15,32,2048]{2,1,0:T(8,128)(2,1)}, bf16[15,32,2048]{2,1,0:T(8,128)(2,1)}, u32[]{:S(2)}, u32[]{:S(2)}) collective-permute-start(bf16[15,32,2048]{2,1,0:T(8,128)(2,1)} %slice.112), channel_id=1, source_target_pairs={{0,1},{1,2},{2,3},{4,5},{5,6},{6,7},{8,9},{9,10},{10,11},{12,13},{... | collective-permute-start | bytes 5898248 | tf_op jit(solution)/shard_map/ppermute | solution.py:11
  164.5 53.3 %all-to-all-start.1 = ((bf16[1,128,256,2,16]{2,4,3,0,1:T(8,128)(2,1)}), bf16[1,128,256,2,16]{2,4,3,0,1:T(8,128)(2,1)S(1)}, u32[]{:S(2)}, u32[]{:S(2)}) async-start(bf16[1,128,256,2,16]{2,4,3,0,1:T(8,128)(2,1)} %copy.30), calls=%async_computation.1 | async-start | bytes 4194304 | tf_op jit(solution)/shard_map/all_to_all | solution.py:80
  219.2 111.4 %all-to-all-start.2 = ((f32[4,1,512]{2,1,0:T(1,128)}), f32[4,1,512]{2,1,0:T(1,128)S(1)}, u32[]{:S(2)}, u32[]{:S(2)}) async-start(f32[4,1,512]{2,1,0:T(1,128)} %reshape.90), calls=%async_computation.2 | async-start | bytes 16384 | tf_op jit(solution)/shard_map/all_to_all | solution.py:86
